TPU v7x, 32 devices: a whole 2x2x4 slice. The times are simulated.
32 devices in a mesh: row: 1, voc: 32 (over z, y, x, core).
Axes of the slice: x: 2, y: 2, z: 4, core: 2. Of those that a mesh axis runs over, the one named last changes fastest.
Arguments:
- hidden_states: bfloat16 [256, 4096], P('row'), may hold values from -72 to 72
- student_head: bfloat16 [4096, 65536], P('row', 'voc'), may hold values from -2 to 2
- teacher_probs: bfloat16 [256, 81920], P('row', 'voc'), may hold values from 9.9658966e-05 to 1
- block_map: int32 [512, 2], replicated, may hold values from 0 to 639, as said below
- context: int32 [4], P('row'), may hold values from 0 to 3
- map_gates: float32 [4, 512, 2], P(None, 'voc'), may hold values from 0.2 to 5
- map_tiles: bfloat16 [512, 2, 128, 128], P('voc'), may hold values from 0.0009994507 to 1
Outputs:
- grad_logits: bfloat16 [256, 65536], P('row', 'voc')
- head_grad: bfloat16 [4096, 65536], P('row', 'voc')
- kl_loss: float32 [], replicated
Inputs may be any that keep to these rules, and one draw needn't show every extreme that they name: `block_map`: in each aligned block of 16 student blocks, at most 2 of the 32 listed ids lie in any one aligned range of 20 teacher blocks, and exactly 2 in one such range.
All inputs are finite; a program needn't handle non-finite values.
Results may differ from a plain program's by a relative error of at most 0.013.
Values may be sent and summed in bfloat16 or wider, within the bound.
A program may use at most 128 MiB of HBM per device.

v0:
```python
import math
import jax
import jax.numpy as jnp
from jax import lax
from jax.sharding import PartitionSpec as P


def map_teacher(teacher_probs, block_map, context, map_gates, map_tiles):
    voc_count = lax.axis_size("voc")
    own_index = lax.axis_index("voc")
    blocks, fanout, block_width, _ = map_tiles.shape
    tokens_here = teacher_probs.shape[0]
    per_shard = teacher_probs.shape[1] // block_width
    entries = blocks * fanout
    capacity = entries // voc_count + 1
    wanted_all = block_map.reshape(voc_count, entries)
    sources_all = wanted_all // per_shard
    owned = (sources_all == own_index).astype(jnp.int32)
    rank_in = jnp.cumsum(owned, axis=1) - 1
    selected = owned[:, None, :] * (
        rank_in[:, None, :] == jnp.arange(capacity)[None, :, None]
    ).astype(jnp.int32)
    local_ids = wanted_all - own_index * per_shard
    take_index = jnp.sum(selected * local_ids[:, None, :], axis=2).reshape(-1)
    filled = jnp.sum(selected, axis=2).reshape(-1) > 0
    teacher_blocks = teacher_probs.reshape(tokens_here, per_shard, block_width)
    outgoing = jnp.where(
        filled[None, :, None],
        jnp.take(teacher_blocks, take_index, axis=1),
        jnp.zeros((), teacher_probs.dtype),
    )
    incoming = lax.all_to_all(outgoing, "voc", split_axis=1, concat_axis=1, tiled=True)
    wanted = lax.dynamic_index_in_dim(wanted_all, own_index, 0, keepdims=False)
    sources = wanted // per_shard
    source_hot = (sources[:, None] == jnp.arange(voc_count)[None, :]).astype(jnp.int32)
    position = jnp.sum(source_hot * (jnp.cumsum(source_hot, axis=0) - 1), axis=1)
    pieces = jnp.take(incoming, sources * capacity + position, axis=1).reshape(
        tokens_here, blocks, fanout, block_width
    )
    products = jnp.einsum("tbkj,bkjc->tbkc", pieces, map_tiles, preferred_element_type=jnp.float32)
    window = tokens_here // context.shape[0]
    token_context = jnp.repeat(context, window)
    context_count = map_gates.shape[0]
    context_hot = (token_context[:, None] == jnp.arange(context_count)[None, :]).astype(jnp.float32)
    gate_token = jnp.dot(
        context_hot, map_gates.reshape(context_count, entries), precision=lax.Precision.HIGHEST
    )
    gate_token = gate_token.reshape(tokens_here, blocks, fanout)
    mapped = jnp.sum(gate_token[..., None] * products, axis=2)
    return mapped.reshape(tokens_here, blocks * block_width)


def per_device(
    hidden_states, student_head, teacher_probs, block_map, context, map_gates, map_tiles
):
    tokens_here = hidden_states.shape[0]
    vocab_cols = student_head.shape[1]
    rows_total = tokens_here * lax.axis_size("row")
    inv_root = 1.0 / math.sqrt(rows_total)
    columns = hidden_states
    logits = jnp.dot(
        columns,
        lax.all_gather(student_head, "row", axis=0, tiled=True),
        preferred_element_type=jnp.float32,
    )
    mapped = map_teacher(teacher_probs, block_map, context, map_gates, map_tiles)
    local_total = jnp.sum(mapped, axis=1)
    peak = lax.pmax(jnp.max(logits, axis=1), "voc")
    summed, row_total = lax.psum(
        (jnp.sum(jnp.exp(logits - peak[:, None]), axis=1), local_total), "voc"
    )
    log_norm = peak + jnp.log(summed)
    target = mapped / row_total[:, None]
    vocab_total = vocab_cols * lax.axis_size("voc")
    grad_logits = (vocab_total * (jnp.exp(logits - log_norm[:, None]) - target)).astype(
        jnp.bfloat16
    )
    kl_partial = jnp.sum(target * (jnp.log(target) - logits + log_norm[:, None]))
    kl_loss = lax.psum(kl_partial, ("row", "voc")) / rows_total
    columns = hidden_states
    head_grad = lax.psum_scatter(
        (
            jnp.einsum("td,tv->dv", columns, grad_logits, preferred_element_type=jnp.float32)
            * inv_root
        ).astype(jnp.bfloat16),
        "row",
        scatter_dimension=0,
        tiled=True,
    )
    return (grad_logits, head_grad, kl_loss)


def solution(mesh):
    placed = (
        P("row", None),
        P("row", "voc"),
        P("row", "voc"),
        P(),
        P("row"),
        P(None, "voc", None),
        P("voc", None, None, None),
    )
    return jax.shard_map(
        per_device,
        mesh=mesh,
        in_specs=placed,
        out_specs=(P("row", "voc"), P("row", "voc"), P()),
        check_vma=False,
    )
```

profile of v0, /device:TPU:0, one launch (start us, length us, event | category | flops | bytes accessed | tf_op | source)
XLA Modules:
  0.0 265.5 jit_solution(6915176413589126362)
XLA Ops:
  0.6 0.0 copy-start
  0.6 1.0 copy.49
  1.6 0.1 reshape.240
  1.8 0.2 reduce_window_sum.23
  2.0 0.2 select_reduce_fusion
  2.2 0.1 copy.56
  2.2 0.1 reshape.243
  2.4 0.1 reshape.241
  2.5 0.1 copy.55
  2.6 0.1 gt.19
  2.7 2.4 copy.57
  5.2 1.8 copy.59
  6.9 3.1 %gather_fusion = bf16[64,256,128]{2,1,0:T(8,128)(2,1)} fusion(bf16[256,20,128]{2,0,1:T(8,128)(2,1)S(1)} %copy.59, s32[1024]{0:T(1024)S(1)} %pad_clamp_fusion.1), kind=kCustom, calls=%fused_computation | custom fusion | bytes 8388864 | tf_op jit(solution)/shard_map/jit(_take)/gather | solution.py:29
  10.0 4.0 %select_bitcast_fusion = bf16[256,64,128]{2,0,1:T(8,128)(2,1)} fusion(bf16[64,256,128]{2,1,0:T(8,128)(2,1)} %gather_fusion, pred[64]{0:T(512)(128)(4,1)S(1)} %gt.19, pred[64]{0:T(512)(128)(4,1)S(1)} %compare_and_fusion), kind=kLoop, calls=%fused_computation.5 | loop fusion | flops 4194304 | bytes 8388736 | tf_op jit(solution)/shard_map/jit(_where)/select_n | solution.py:27
  14.0 0.0 copy-start.2
  14.0 0.0 copy-start.4
  14.0 7.4 %all-to-all-start = ((bf16[256,64,128]{2,0,1:T(8,128)(2,1)}), bf16[256,64,128]{2,0,1:T(8,128)(2,1)}, u32[]{:S(2)}, u32[]{:S(2)}) async-start(bf16[256,64,128]{2,0,1:T(8,128)(2,1)} %select_bitcast_fusion), calls=%async_computation | async-start | bytes 8388608 | tf_op jit(solution)/shard_map/all_to_all | solution.py:32
  21.5 0.0 copy-done.2
  21.5 0.1 broadcast_in_dim.47
  21.6 0.1 eq.55
  21.6 0.0 copy-done.4
  21.6 0.2 fusion.12
  21.9 0.5 broadcast.277
  22.4 0.7 fusion.25
  23.1 0.1 and.55
  23.2 0.1 copy.51
  23.3 0.5 broadcast.278
  23.8 0.7 fusion.24
  24.5 0.1 div.54
  24.6 0.1 copy.50
  24.7 0.1 fusion.9
  24.7 0.1 reduce_window_sum.22
  24.8 0.2 select_reduce_fusion.1
  25.0 0.1 reduce_sum.69
  25.1 0.1 copy.53
  25.2 0.1 copy.54
  25.3 0.0 copy-done
  25.3 9.6 %fusion.26 = (f32[256]{0:T(256)S(1)}, f32[256,2048]{1,0:T(8,128)}) fusion(bf16[256,4096]{1,0:T(8,128)(2,1)S(1)} %copy-done, bf16[4096,2048]{1,0:T(8,128)(2,1)} %param.8), kind=kOutput, calls=%fused_computation.61 | convolution fusion | flops 4295491584 | bytes 20972544 | tf_op jit(solution)/shard_map/dot_general | solution.py:61
  34.9 100.9 %pmax.7 = f32[256]{0:T(256)S(1)} all-reduce(f32[256]{0:T(256)S(1)} %get-tuple-element.30), channel_id=1, replica_groups=mesh['row'=1,'voc'=32] {'voc'}, use_global_device_ids=true, to_apply=%region_1.2 | all-reduce | flops 256 | bytes 2048 | tf_op jit(solution)/shard_map/pmax | solution.py:68
  135.8 2.0 exponential_reduce_fusion
  137.8 0.0 copy-start.3
  137.8 0.0 all-to-all-done
  137.8 4.4 %gather_fusion.1 = bf16[32,256,128]{2,1,0:T(8,128)(2,1)} fusion(bf16[256,64,128]{2,0,1:T(8,128)(2,1)} %all-to-all-done, s32[1024]{0:T(1024)S(1)} %pad_clamp_fusion), kind=kCustom, calls=%fused_computation.1 | custom fusion | bytes 4194432 | tf_op jit(solution)/shard_map/jit(_take)/gather | solution.py:37
  142.2 0.0 copy-done.3
  142.2 4.0 %fusion.1 = (f32[256]{0:T(256)S(1)}, f32[256,16,128]{0,2,1:T(8,128)}) fusion(f32[256,16,2]{0,2,1:T(2,128)S(1)} %copy.48, bf16[16,2,128,128]{3,2,1,0:T(8,128)(2,1)S(1)} %copy-done.3, bf16[256,16,2,128]{3,0,2,1:T(8,128)(2,1)} %bitcast.52, pred[16,2]{1,0:T(8,128)(4,1)S(1)} %copy.54), kind=kOutput, calls=%fused_computation.6 | convolution fusion | flops 272105216 | bytes 5276704 | tf_op jit(solution)/shard_map/tbkj,bkjc->tbkc/dot_general | solution.py:40
  146.2 2.9 %copy.65 = f32[256,2048]{1,0:T(8,128)} copy(f32[256,2048]{0,1:T(8,128)} %bitcast.53) | data formatting | bytes 4194304 | tf_op jit(solution)/shard_map/reshape | solution.py:50
  149.1 38.1 %all-reduce = (f32[256]{0:T(256)S(1)}, f32[256]{0:T(256)S(1)}) all-reduce(f32[256]{0:T(256)S(1)} %exponential_reduce_fusion, f32[256]{0:T(256)S(1)} %get-tuple-element.18), channel_id=1, replica_groups=mesh['row'=1,'voc'=32] {'voc'}, use_global_device_ids=true, to_apply=%region_3.4 | all-reduce | flops 512 | bytes 4096 | tf_op jit(solution)/shard_map/psum | solution.py:69
  187.2 3.8 %multiply_reduce_fusion = (f32[]{:T(128)}, bf16[256,2048]{1,0:T(8,128)(2,1)S(1)}) fusion(f32[256,2048]{1,0:T(8,128)} %get-tuple-element.31, f32[256]{0:T(256)S(1)} %log_add_fusion, f32[256,2048]{1,0:T(8,128)} %copy.65, f32[256]{0:T(256)S(1)} %get-tuple-element.23), kind=kLoop, calls=%fused_computation.8 | loop fusion | flops 4718591 | bytes 5244932 | tf_op jit(solution)/shard_map/reduce_sum | solution.py:78
  191.0 0.0 copy-start.1
  191.0 42.2 %psum.23 = f32[]{:T(128)} all-reduce(f32[]{:T(128)} %get-tuple-element.28), channel_id=1, replica_groups=mesh['row'=1,'voc'=32] {'row','voc'}, use_global_device_ids=true, to_apply=%region_13.14 | all-reduce | flops 1 | bytes 8 | tf_op jit(solution)/shard_map/psum | solution.py:79
  233.3 8.1 %fusion = bf16[4096,2048]{0,1:T(8,128)(2,1)} fusion(bf16[256,2048]{1,0:T(8,128)(2,1)S(1)} %get-tuple-element.29, bf16[256,4096]{1,0:T(8,128)(2,1)S(1)} %copy-done), kind=kOutput, calls=%fused_computation.3 | convolution fusion | flops 4311744512 | bytes 19922944 | tf_op jit(solution)/shard_map/td,tv->dv/dot_general | solution.py:83
  241.3 0.0 copy-done.1
  241.3 22.4 %copy.62 = bf16[4096,2048]{1,0:T(8,128)(2,1)} copy(bf16[4096,2048]{0,1:T(8,128)(2,1)} %fusion) | data formatting | bytes 33554432
  (12 shorter events, 0.1 us)
Async XLA Ops:
  0.6 24.6 %copy-start = (bf16[256,4096]{1,0:T(8,128)(2,1)S(1)}, bf16[256,4096]{1,0:T(8,128)(2,1)}, u32[]{:S(2)}) copy-start(bf16[256,4096]{1,0:T(8,128)(2,1)} %param.7) | copy-start | bytes 6291460
  14.0 7.4 %copy-start.2 = (s32[4]{0:T(128)S(1)}, s32[4]{0:T(128)}, u32[]{:S(2)}) copy-start(s32[4]{0:T(128)} %param.11) | copy-start | bytes 52
  14.0 7.6 %copy-start.4 = (f32[4,16,2]{1,2,0:T(2,128)S(1)}, f32[4,16,2]{1,2,0:T(2,128)}, u32[]{:S(2)}) copy-start(f32[4,16,2]{1,2,0:T(2,128)} %param.12) | copy-start | bytes 1540
  14.0 123.8 %all-to-all-start = ((bf16[256,64,128]{2,0,1:T(8,128)(2,1)}), bf16[256,64,128]{2,0,1:T(8,128)(2,1)}, u32[]{:S(2)}, u32[]{:S(2)}) async-start(bf16[256,64,128]{2,0,1:T(8,128)(2,1)} %select_bitcast_fusion), calls=%async_computation | async-start | bytes 8388608 | tf_op jit(solution)/shard_map/all_to_all | solution.py:32
  137.8 4.4 %copy-start.3 = (bf16[16,2,128,128]{3,2,1,0:T(8,128)(2,1)S(1)}, bf16[16,2,128,128]{3,2,1,0:T(8,128)(2,1)}, u32[]{:S(2)}) copy-start(bf16[16,2,128,128]{3,2,1,0:T(8,128)(2,1)} %param.13) | copy-start | bytes 3145732
  191.0 50.3 %copy-start.1 = (bf16[256,2048]{1,0:T(8,128)(2,1)}, bf16[256,2048]{1,0:T(8,128)(2,1)S(1)}, u32[]{:S(2)}) copy-start(bf16[256,2048]{1,0:T(8,128)(2,1)S(1)} %get-tuple-element.29) | copy-start | bytes 3145732
where the time goes:
time: 267 us; the launch traced here: 266 us
  blocking collectives  181 us (68%)
  local copies, waits for them, and re-layouts  40.5 us (15%)
  matrix products  21.9 us (8%)
  other arithmetic  12 us (4%)
  starting transfers between devices  7.43 us (3%)
    pmax x1, blocking collectives, per_device(): peak = lax.pmax(jnp.max(logits, axis=1), 'voc')  101 us
    psum x1, blocking collectives, per_device(): kl_loss = lax.psum(kl_partial, ('row', 'voc')) / rows_total  42.2 us
    psum x1, blocking collectives, per_device(): lax.psum((jnp.sum(jnp.exp(logits - peak[:, None]), axis=1), local_total),...  38.1 us
    unnamed x13, local copies, waits for them, and re-layouts  25.9 us
    dot_general x1, matrix products, per_device(): jnp.dot(columns, lax.all_gather(student_head, 'row', axis=0, tiled=True),...  9.62 us
    dot_general x1, matrix products, per_device(): jnp.einsum('td,tv->dv', columns, grad_logits, preferred_element_type=jnp....  8.08 us
    all_to_all x1, starting transfers between devices, map_teacher(): lax.all_to_all(outgoing, 'voc', split_axis=1, concat_axis=1, tiled=True)  7.43 us
  transfers between devices with their start and end apart: 1, of which 0 were waited for; matrix products, arithmetic and copies ran while one was open for 6% of the time, Pallas kernels for 0%

commit v1 on v0

--- a/solution.py
+++ b/solution.py
@@ -29,7 +29,10 @@
         jnp.take(teacher_blocks, take_index, axis=1),
         jnp.zeros((), teacher_probs.dtype),
     )
-    incoming = lax.all_to_all(outgoing, "voc", split_axis=1, concat_axis=1, tiled=True)
+    incoming = jnp.concatenate(
+        lax.all_to_all(jnp.stack(jnp.split(outgoing, lax.axis_size("voc"), axis=1)), "voc", 0, 0),
+        axis=1,
+    )
     wanted = lax.dynamic_index_in_dim(wanted_all, own_index, 0, keepdims=False)
     sources = wanted // per_shard
     source_hot = (sources[:, None] == jnp.arange(voc_count)[None, :]).astype(jnp.int32)

time: 267 us -> 286 us (1.071)
  local copies, waits for them, and re-layouts: 40.5 us -> 61.7 us
    unnamed x13 -> x44, local copies, waits for them, and re-layouts: 25.9 us -> 46.4 us
  transfers between devices with their start and end apart: 1 -> 1, of which waited for: 0 -> 0; matrix products, arithmetic and copies ran while one was open for 6% -> 5% of each run, Pallas kernels for 0% -> 0%
where the time goes in v1:
time: 286 us; the launch traced here: 285 us
  blocking collectives  181 us (63%)
  local copies, waits for them, and re-layouts  61.7 us (22%)
  matrix products  21.9 us (8%)
  other arithmetic  10.6 us (4%)
  starting transfers between devices  7.43 us (3%)
    pmax x1, blocking collectives, per_device(): peak = lax.pmax(jnp.max(logits, axis=1), 'voc')  101 us
    unnamed x44, local copies, waits for them, and re-layouts  46.4 us
    psum x1, blocking collectives, per_device(): kl_loss = lax.psum(kl_partial, ('row', 'voc')) / rows_total  42.2 us
    psum x1, blocking collectives, per_device(): lax.psum((jnp.sum(jnp.exp(logits - peak[:, None]), axis=1), local_total),...  38.1 us
    dot_general x1, matrix products, per_device(): jnp.dot(columns, lax.all_gather(student_head, 'row', axis=0, tiled=True),...  9.62 us
    dot_general x1, matrix products, per_device(): jnp.einsum('td,tv->dv', columns, grad_logits, preferred_element_type=jnp....  8.08 us
    all_to_all x1, starting transfers between devices, map_teacher(): lax.all_to_all(jnp.stack(jnp.split(outgoing, lax.axis_size('voc'), axis=1...  7.43 us
  transfers between devices with their start and end apart: 1, of which 0 were waited for; matrix products, arithmetic and copies ran while one was open for 5% of the time, Pallas kernels for 0%

profile of v1, /device:TPU:0, one launch (start us, length us, event | category | flops | bytes accessed | tf_op | source)
XLA Modules:
  0.0 285.4 jit_solution(7378014420723336388)
XLA Ops:
  0.6 1.0 copy.48
  1.6 0.1 reshape.246
  1.8 0.2 reduce_window_sum.23
  2.0 0.2 select_reduce_fusion
  2.2 0.1 reshape.249
  2.4 0.1 reshape.247
  2.5 0.1 copy.54
  2.6 0.1 gt.19
  2.7 2.4 copy.56
  5.2 1.8 copy.58
  6.9 3.1 %gather_fusion = bf16[64,256,128]{2,1,0:T(8,128)(2,1)} fusion(bf16[256,20,128]{2,0,1:T(8,128)(2,1)S(1)} %copy.58, s32[1024]{0:T(1024)S(1)} %pad_clamp_fusion.1), kind=kCustom, calls=%fused_computation | custom fusion | bytes 8388864 | tf_op jit(solution)/shard_map/jit(_take)/gather | solution.py:29
  10.0 2.7 select_bitcast_fusion
  12.7 0.7 fusion.38
  13.4 0.7 fusion.37
  14.0 0.7 fusion.36
  14.7 0.7 fusion.35
  15.4 0.7 fusion.34
  16.0 0.7 fusion.33
  16.7 0.7 fusion.32
  17.3 0.7 fusion.31
  18.0 0.7 fusion.30
  18.7 0.7 fusion.29
  19.3 0.7 fusion.28
  20.0 0.7 fusion.27
  20.7 0.7 fusion.26
  21.3 0.7 fusion.25
  22.0 0.7 fusion.24
  22.7 0.7 fusion.23
  23.3 0.7 fusion.22
  24.0 0.7 fusion.21
  24.7 0.7 fusion.20
  25.3 0.7 fusion.19
  26.0 0.7 fusion.18
  26.6 0.7 fusion.17
  27.3 0.7 fusion.16
  28.0 0.7 fusion.15
  28.6 0.7 fusion.14
  29.3 0.7 fusion.13
  30.0 0.7 fusion.12
  30.6 0.7 fusion.11
  31.3 0.7 fusion.10
  32.0 0.7 fusion.9
  32.6 0.7 fusion.8
  33.3 0.7 fusion.7
  34.0 7.4 %all-to-all-start = ((bf16[32,256,2,128]{3,1,2,0:T(8,128)(2,1)}), bf16[32,256,2,128]{3,1,2,0:T(8,128)(2,1)}, u32[]{:S(2)}, u32[]{:S(2)}) async-start(bf16[32,256,2,128]{3,1,2,0:T(8,128)(2,1)} %fusion.7), calls=%async_computation | async-start | bytes 8388608 | tf_op jit(solution)/shard_map/all_to_all | solution.py:33
  41.6 0.2 fusion.44
  41.8 0.5 broadcast.277
  42.3 0.7 fusion.57
  43.1 0.1 copy.50
  43.2 0.5 broadcast.278
  43.7 0.7 fusion.56
  44.7 0.2 select_reduce_fusion.1
  45.1 0.1 copy.53
  45.2 9.6 %fusion.58 = (f32[256]{0:T(256)S(1)}, f32[256,2048]{1,0:T(8,128)}) fusion(bf16[256,4096]{1,0:T(8,128)(2,1)S(1)} %copy-done, bf16[4096,2048]{1,0:T(8,128)(2,1)} %param.8), kind=kOutput, calls=%fused_computation.125 | convolution fusion | flops 4295491584 | bytes 20972544 | tf_op jit(solution)/shard_map/dot_general | solution.py:64
  54.8 100.9 %pmax.7 = f32[256]{0:T(256)S(1)} all-reduce(f32[256]{0:T(256)S(1)} %get-tuple-element.30), channel_id=1, replica_groups=mesh['row'=1,'voc'=32] {'voc'}, use_global_device_ids=true, to_apply=%region_1.2 | all-reduce | flops 256 | bytes 2048 | tf_op jit(solution)/shard_map/pmax | solution.py:71
  155.7 2.0 exponential_reduce_fusion
  157.7 4.3 %gather_fusion.1 = bf16[32,256,128]{2,1,0:T(8,128)(2,1)} fusion(bf16[256,64,128]{2,0,1:T(8,128)(2,1)} %bitcast.43, s32[1024]{0:T(1024)S(1)} %pad_clamp_fusion), kind=kCustom, calls=%fused_computation.1 | custom fusion | bytes 4194432 | tf_op jit(solution)/shard_map/jit(_take)/gather | solution.py:40
  162.0 4.0 %fusion.1 = (f32[256]{0:T(256)S(1)}, f32[256,16,128]{0,2,1:T(8,128)}) fusion(f32[256,16,2]{0,2,1:T(2,128)S(1)} %copy.47, bf16[16,2,128,128]{3,2,1,0:T(8,128)(2,1)S(1)} %copy-done.3, bf16[256,16,2,128]{3,0,2,1:T(8,128)(2,1)} %bitcast.183, pred[16,2]{1,0:T(8,128)(4,1)S(1)} %copy.53), kind=kOutput, calls=%fused_computation.6 | convolution fusion | flops 272105216 | bytes 5276704 | tf_op jit(solution)/shard_map/tbkj,bkjc->tbkc/dot_general | solution.py:43
  166.0 2.9 %copy.64 = f32[256,2048]{1,0:T(8,128)} copy(f32[256,2048]{0,1:T(8,128)} %bitcast.184) | data formatting | bytes 4194304 | tf_op jit(solution)/shard_map/reshape | solution.py:53
  168.9 38.1 %all-reduce = (f32[256]{0:T(256)S(1)}, f32[256]{0:T(256)S(1)}) all-reduce(f32[256]{0:T(256)S(1)} %exponential_reduce_fusion, f32[256]{0:T(256)S(1)} %get-tuple-element.18), channel_id=1, replica_groups=mesh['row'=1,'voc'=32] {'voc'}, use_global_device_ids=true, to_apply=%region_3.4 | all-reduce | flops 512 | bytes 4096 | tf_op jit(solution)/shard_map/psum | solution.py:72
  207.0 3.8 %multiply_reduce_fusion = (f32[]{:T(128)}, bf16[256,2048]{1,0:T(8,128)(2,1)S(1)}) fusion(f32[256,2048]{1,0:T(8,128)} %get-tuple-element.31, f32[256]{0:T(256)S(1)} %log_add_fusion, f32[256,2048]{1,0:T(8,128)} %copy.64, f32[256]{0:T(256)S(1)} %get-tuple-element.23), kind=kLoop, calls=%fused_computation.8 | loop fusion | flops 4718591 | bytes 5244932 | tf_op jit(solution)/shard_map/reduce_sum | solution.py:81
  210.9 42.2 %psum.23 = f32[]{:T(128)} all-reduce(f32[]{:T(128)} %get-tuple-element.28), channel_id=1, replica_groups=mesh['row'=1,'voc'=32] {'row','voc'}, use_global_device_ids=true, to_apply=%region_13.14 | all-reduce | flops 1 | bytes 8 | tf_op jit(solution)/shard_map/psum | solution.py:82
  253.1 8.1 %fusion = bf16[4096,2048]{0,1:T(8,128)(2,1)} fusion(bf16[256,2048]{1,0:T(8,128)(2,1)S(1)} %get-tuple-element.29, bf16[256,4096]{1,0:T(8,128)(2,1)S(1)} %copy-done), kind=kOutput, calls=%fused_computation.3 | convolution fusion | flops 4311744512 | bytes 19922944 | tf_op jit(solution)/shard_map/td,tv->dv/dot_general | solution.py:86
  261.1 22.4 %copy.61 = bf16[4096,2048]{1,0:T(8,128)(2,1)} copy(bf16[4096,2048]{0,1:T(8,128)(2,1)} %fusion) | data formatting | bytes 33554432
  (33 shorter events, 1.0 us)
Async XLA Ops:
  0.6 44.6 %copy-start = (bf16[256,4096]{1,0:T(8,128)(2,1)S(1)}, bf16[256,4096]{1,0:T(8,128)(2,1)}, u32[]{:S(2)}) copy-start(bf16[256,4096]{1,0:T(8,128)(2,1)} %param.7) | copy-start | bytes 6291460
  34.0 7.4 %copy-start.2 = (s32[4]{0:T(128)S(1)}, s32[4]{0:T(128)}, u32[]{:S(2)}) copy-start(s32[4]{0:T(128)} %param.11) | copy-start | bytes 52
  34.0 7.6 %copy-start.4 = (f32[4,16,2]{1,2,0:T(2,128)S(1)}, f32[4,16,2]{1,2,0:T(2,128)}, u32[]{:S(2)}) copy-start(f32[4,16,2]{1,2,0:T(2,128)} %param.12) | copy-start | bytes 1540
  34.0 123.7 %all-to-all-start = ((bf16[32,256,2,128]{3,1,2,0:T(8,128)(2,1)}), bf16[32,256,2,128]{3,1,2,0:T(8,128)(2,1)}, u32[]{:S(2)}, u32[]{:S(2)}) async-start(bf16[32,256,2,128]{3,1,2,0:T(8,128)(2,1)} %fusion.7), calls=%async_computation | async-start | bytes 8388608 | tf_op jit(solution)/shard_map/all_to_all | solution.py:33
  54.8 107.2 %copy-start.3 = (bf16[16,2,128,128]{3,2,1,0:T(8,128)(2,1)S(1)}, bf16[16,2,128,128]{3,2,1,0:T(8,128)(2,1)}, u32[]{:S(2)}) copy-start(bf16[16,2,128,128]{3,2,1,0:T(8,128)(2,1)} %param.13) | copy-start | bytes 3145732
  210.9 50.3 %copy-start.1 = (bf16[256,2048]{1,0:T(8,128)(2,1)}, bf16[256,2048]{1,0:T(8,128)(2,1)S(1)}, u32[]{:S(2)}) copy-start(bf16[256,2048]{1,0:T(8,128)(2,1)S(1)} %get-tuple-element.29) | copy-start | bytes 3145732
